TPU v7x, 256 devices: a whole 4x4x8 slice. The times are simulated.
256 devices in a mesh: seg: 8 (over x, y_hi), gx: 2 (over y_lo), gz: 16 (over z, core).
Axes of the slice: x: 4, y: 4 (y_hi: 2, y_lo: 2; y = y_hi * 2 + y_lo), z: 8, core: 2. Of those that a mesh axis runs over, the one named last changes fastest.
Arguments:
- terminal: float32 [8, 3, 128, 256, 256], P('seg', None, 'gx', 'gz'), may hold values from -6 to 6
- jump: float32 [8, 3, 128, 256, 256], P('seg', None, 'gx', 'gz'), may hold values from -61 to 61
- tangent: float32 [8, 3, 128, 256, 256], P('seg', None, 'gx', 'gz'), may hold values from -36 to 36
- base_velocity: float32 [256], replicated, may hold values from 0.5 to 2
- base_shear: float32 [256], replicated, may hold values from -2 to 2
Outputs:
- adjoint_field: float32 [8, 3, 128, 256, 256], P('seg', None, 'gx', 'gz')
All inputs are finite; a program needn't handle non-finite values. Where the computation divides by a largest or mean magnitude, that divisor is 1e-20 or more.
Results may differ from a plain program's by a relative error of at most 0.00018.
Values sent between devices are 32-bit elements; how exact they have to be, the bound alone decides.
A program may use at most 64 MiB of HBM per device.

v0:
```python
import jax
import jax.numpy as jnp
import numpy as np
from jax import lax
from jax.sharding import PartitionSpec as P

STEPS = 4
TIME_STEP = 0.15
DIFFUSE = 0.1
WALL_COEF = 0.0002
EPSILON = 1e-06
NEWTON_TURNS = 100


def with_halo(cells, sides, width):
    for axis, dim in sides:
        count = lax.axis_size(axis)
        head = lax.slice_in_dim(cells, 0, width, axis=dim)
        tail = lax.slice_in_dim(cells, cells.shape[dim] - width, cells.shape[dim], axis=dim)
        cells = jnp.concatenate(
            [
                lax.ppermute(tail, axis, [(i, (i + 1) % count) for i in range(count)]),
                cells,
                lax.ppermute(head, axis, [((i + 1) % count, i) for i in range(count)]),
            ],
            axis=dim,
        )
    return cells


def from_behind(value, axis, steps):
    count = lax.axis_size(axis)
    pairs = [(source, (source + steps) % count) for source in range(count)]
    return lax.ppermute(value, axis, pairs)


def invert_newton(matrix):
    order = matrix.shape[0]
    identity = np.eye(order)
    scale_one = np.max(np.sum(np.abs(matrix), axis=0))
    scale_inf = np.max(np.sum(np.abs(matrix), axis=1))
    approx = matrix.T / (scale_one * scale_inf)
    for turn_index in range(NEWTON_TURNS):
        approx = approx @ (2.0 * identity - matrix @ approx)
    return approx


def wall_table(points):
    intervals = points - 1
    cheb_nodes = np.cos(np.pi * np.arange(points) / intervals)
    weights = np.ones(points)
    weights[0] = 2.0
    weights[-1] = 2.0
    weights = weights * (-1.0) ** np.arange(points)
    spread = cheb_nodes[:, None] - cheb_nodes[None, :]
    first_deriv = weights[:, None] / weights[None, :] / (spread + np.eye(points))
    first_deriv = first_deriv - np.eye(points) * first_deriv.sum(axis=1)[:, None]
    second = first_deriv @ first_deriv
    interior = np.eye(points - 2) - WALL_COEF * second[1:-1, 1:-1]
    helm_table = np.zeros((points, points))
    helm_table[1:-1, 1:-1] = invert_newton(interior)
    return jnp.asarray(helm_table.T, dtype=jnp.float32)


def advance(padded, velocity, shear, table_t):
    center = padded[:, 2:-2, 2:-2, :]
    fwd2_x = padded[:, 4:, 2:-2, :]
    fwd1_x = padded[:, 3:-1, 2:-2, :]
    back1_x = padded[:, 1:-3, 2:-2, :]
    back2_x = padded[:, :-4, 2:-2, :]
    fwd2_z = padded[:, 2:-2, 4:, :]
    fwd1_z = padded[:, 2:-2, 3:-1, :]
    back1_z = padded[:, 2:-2, 1:-3, :]
    back2_z = padded[:, 2:-2, :-4, :]
    advect = (back2_x - fwd2_x + 8.0 * (fwd1_x - back1_x)) / 12.0
    lap_x = (16.0 * (fwd1_x + back1_x) - (fwd2_x + back2_x) - 30.0 * center) / 12.0
    lap_z = (16.0 * (fwd1_z + back1_z) - (fwd2_z + back2_z) - 30.0 * center) / 12.0
    explicit = center + TIME_STEP * velocity * advect + DIFFUSE * (lap_x + lap_z)
    explicit = jnp.concatenate(
        [explicit[:1], explicit[1:2] - TIME_STEP * shear * center[:1], explicit[2:]], axis=0
    )
    flattened = explicit.reshape(-1, explicit.shape[-1])
    updated = jnp.dot(
        flattened, table_t, precision=lax.Precision.HIGHEST, preferred_element_type=jnp.float32
    )
    return updated.reshape(explicit.shape)


def extend(adjoint, width):
    along_x = with_halo(adjoint, (("gx", 1),), width)
    return with_halo(along_x, (("gz", 2),), width)


def shards(terminal, jump, tangent, base_velocity, base_shear):
    table_t = wall_table(base_velocity.shape[0])
    received = from_behind(terminal, "seg", -1)
    started = received[0] + jump[0]
    direction = tangent[0]
    products = lax.psum(
        (jnp.sum(started * direction), jnp.sum(direction * direction)), ("gx", "gz")
    )
    along_coef = products[0] / (products[1] + EPSILON)
    adjoint = started - along_coef * direction
    for step_index in range(STEPS):
        padded = extend(adjoint, 2)
        adjoint = advance(padded, base_velocity, base_shear, table_t)
    return adjoint[None]


def solution(mesh):
    in_specs = (
        P("seg", None, "gx", "gz", None),
        P("seg", None, "gx", "gz", None),
        P("seg", None, "gx", "gz", None),
        P(),
        P(),
    )
    out_specs = P("seg", None, "gx", "gz", None)
    return jax.shard_map(shards, mesh=mesh, in_specs=in_specs, out_specs=out_specs, check_vma=False)
```

profile of v0, /device:TPU:22, one launch (start us, length us, event | category | flops | bytes accessed | tf_op | source)
XLA Modules:
  0.0 248.8 jit_solution(7663834592041668082)
XLA Ops:
  0.3 73.3 %collective-permute-done = f32[1,3,64,16,256]{4,3,2,1,0:T(8,128)S(1)} collective-permute-done((f32[1,3,64,16,256]{4,3,2,1,0:T(8,128)}, f32[1,3,64,16,256]{4,3,2,1,0:T(8,128)S(1)}, u32[]{:S(2)}, u32[]{:S(2)}) %collective-permute-start) | collective-permute-done | bytes 3145760 | tf_op jit(solution)/shard_map/ppermute | solution.py:34
  73.7 5.4 %fusion.39 = (f32[]{:T(128)}, f32[]{:T(128)}) fusion(f32[1,3,64,16,256]{4,3,2,1,0:T(8,128)} %param.8, f32[1,3,64,16,256]{4,3,2,1,0:T(8,128)S(1)} %collective-permute-done, f32[1,3,64,16,256]{4,3,2,1,0:T(8,128)} %param.7), kind=kLoop, calls=%fused_computation.85 | loop fusion | flops 3932158 | bytes 9437192 | tf_op jit(solution)/shard_map/reduce_sum | solution.py:100
  79.1 58.7 %all-reduce = (f32[]{:T(128)}, f32[]{:T(128)}) all-reduce(f32[]{:T(128)} %get-tuple-element.6, f32[]{:T(128)} %get-tuple-element.5), channel_id=1, replica_groups=mesh['seg'=8,'gx'=2,'gz'=16] {'gx','gz'}, use_global_device_ids=true, to_apply=%region_1.0 | all-reduce | flops 2 | bytes 16 | tf_op jit(solution)/shard_map/psum | solution.py:99
  139.2 4.0 %fusion.40 = f32[3,64,16,256]{3,2,1,0:T(8,128)S(1)} fusion(f32[1,3,64,16,256]{4,3,2,1,0:T(8,128)S(1)} %copy-done, f32[]{:T(128)S(6)} %div.31, f32[1,3,64,16,256]{4,3,2,1,0:T(8,128)} %copy-done.1, f32[1,3,64,16,256]{4,3,2,1,0:T(8,128)} %param.7), kind=kLoop, calls=%fused_computation.86 | loop fusion | flops 2359296 | bytes 12582916 | tf_op jit(solution)/shard_map/sub | solution.py:103
  143.2 0.8 collective-permute-start.1
  144.0 1.3 collective-permute-start.2
  145.3 2.6 %collective-permute-done.1 = f32[3,2,16,256]{3,2,1,0:T(8,128)S(1)} collective-permute-done((f32[3,2,16,256]{3,2,1,0:T(8,128)S(1)}, f32[3,2,16,256]{3,2,1,0:T(8,128)S(1)}, u32[]{:S(2)}, u32[]{:S(2)}) %collective-permute-start.1) | collective-permute-done | bytes 98336 | tf_op jit(solution)/shard_map/ppermute | solution.py:22
  147.9 1.1 collective-permute-done.2
  149.3 0.5 collective-permute-start.4
  149.8 5.0 %collective-permute-done.3 = f32[3,68,2,256]{3,2,1,0:T(2,128)S(1)} collective-permute-done((f32[3,68,2,256]{3,2,1,0:T(2,128)S(1)}, f32[3,68,2,256]{3,2,1,0:T(2,128)S(1)}, u32[]{:S(2)}, u32[]{:S(2)}) %collective-permute-start.3) | collective-permute-done | bytes 417824 | tf_op jit(solution)/shard_map/ppermute | solution.py:24
  154.8 3.1 %collective-permute-done.4 = f32[3,68,2,256]{3,2,1,0:T(2,128)S(1)} collective-permute-done((f32[3,68,2,256]{3,2,1,0:T(2,128)S(1)}, f32[3,68,2,256]{3,2,1,0:T(2,128)S(1)}, u32[]{:S(2)}, u32[]{:S(2)}) %collective-permute-start.4) | collective-permute-done | bytes 417824 | tf_op jit(solution)/shard_map/ppermute | solution.py:22
  158.0 1.3 pad_maximum_fusion
  159.3 4.1 %fusion.30 = f32[3,64,16,256]{3,2,1,0:T(8,128)} fusion(f32[3,68,18,256]{3,2,1,0:T(8,128)S(1)} %get-tuple-element.22, f32[3,68,18,256]{3,2,1,0:T(8,128)S(1)} %get-tuple-element.21, f32[3,64,16,256]{3,2,1,0:T(8,128)S(1)} %fusion.40, f32[3,2,16,256]{3,2,1,0:T(8,128)S(1)} %collective-permute-done.2, f32[3,2,16,256]{3,2,1,0:T(8,128)S(1)} %collective-permute-done.1, ...), kind=kLoop, calls=%fused_computation.67 | loop fusion | flops 18874368 | bytes 19072000 | tf_op jit(solution)/shard_map/add | solution.py:78
  163.4 2.3 fusion.52
  166.0 0.6 copy-done.2
  166.7 2.6 %fusion.54 = f32[3072,256]{1,0:T(8,128)S(1)} fusion(f32[3072,256]{1,0:T(8,128)S(1)} %bitcast.47, f32[256,256]{1,0:T(8,128)S(1)} %copy-done.2), kind=kOutput, calls=%fused_computation.116 | convolution fusion | flops 2415919104 | bytes 6553600 | tf_op jit(solution)/shard_map/dot_general | solution.py:83
  169.3 1.1 collective-permute-start.5
  170.4 1.1 collective-permute-start.6
  171.4 2.6 %collective-permute-done.5 = f32[3,2,16,256]{3,2,1,0:T(8,128)S(1)} collective-permute-done((f32[3,2,16,256]{3,2,1,0:T(8,128)S(1)}, f32[3,2,16,256]{3,2,1,0:T(8,128)S(1)}, u32[]{:S(2)}, u32[]{:S(2)}) %collective-permute-start.5) | collective-permute-done | bytes 98336 | tf_op jit(solution)/shard_map/ppermute | solution.py:22
  174.0 1.1 collective-permute-done.6
  175.4 0.5 collective-permute-start.8
  176.0 5.0 %collective-permute-done.7 = f32[3,68,2,256]{3,2,1,0:T(2,128)S(1)} collective-permute-done((f32[3,68,2,256]{3,2,1,0:T(2,128)S(1)}, f32[3,68,2,256]{3,2,1,0:T(2,128)S(1)}, u32[]{:S(2)}, u32[]{:S(2)}) %collective-permute-start.7) | collective-permute-done | bytes 417824 | tf_op jit(solution)/shard_map/ppermute | solution.py:24
  181.0 3.1 %collective-permute-done.8 = f32[3,68,2,256]{3,2,1,0:T(2,128)S(1)} collective-permute-done((f32[3,68,2,256]{3,2,1,0:T(2,128)S(1)}, f32[3,68,2,256]{3,2,1,0:T(2,128)S(1)}, u32[]{:S(2)}, u32[]{:S(2)}) %collective-permute-start.8) | collective-permute-done | bytes 417824 | tf_op jit(solution)/shard_map/ppermute | solution.py:22
  184.1 1.3 pad_maximum_fusion.1
  185.4 5.0 %fusion.24 = f32[3,64,16,256]{3,2,1,0:T(8,128)} fusion(f32[3,68,18,256]{3,2,1,0:T(8,128)S(1)} %get-tuple-element.18, f32[3,68,18,256]{3,2,1,0:T(8,128)S(1)} %get-tuple-element.17, f32[3,64,16,256]{3,2,1,0:T(8,128)S(1)} %bitcast.41, f32[3,2,16,256]{3,2,1,0:T(8,128)} %copy-done.3, f32[3,2,16,256]{3,2,1,0:T(8,128)S(1)} %collective-permute-done.5, ...), kind=kLoop, calls=%fused_computation.57 | loop fusion | flops 18874368 | bytes 19072000 | tf_op jit(solution)/shard_map/add | solution.py:78
  190.4 2.3 fusion.50
  193.0 2.6 %fusion.55 = f32[3072,256]{1,0:T(8,128)S(1)} fusion(f32[3072,256]{1,0:T(8,128)S(1)} %bitcast.48, f32[256,256]{1,0:T(8,128)S(1)} %copy-done.2), kind=kOutput, calls=%fused_computation.117 | convolution fusion | flops 2415919104 | bytes 6553600 | tf_op jit(solution)/shard_map/dot_general | solution.py:83
  195.7 1.1 collective-permute-start.10
  196.8 1.1 collective-permute-start.9
  197.8 2.6 %collective-permute-done.10 = f32[3,2,16,256]{3,2,1,0:T(8,128)S(1)} collective-permute-done((f32[3,2,16,256]{3,2,1,0:T(8,128)S(1)}, f32[3,2,16,256]{3,2,1,0:T(8,128)S(1)}, u32[]{:S(2)}, u32[]{:S(2)}) %collective-permute-start.10) | collective-permute-done | bytes 98336 | tf_op jit(solution)/shard_map/ppermute | solution.py:24
  200.4 1.1 collective-permute-done.9
  201.8 0.5 collective-permute-start.12
  202.3 5.0 %collective-permute-done.11 = f32[3,68,2,256]{3,2,1,0:T(2,128)S(1)} collective-permute-done((f32[3,68,2,256]{3,2,1,0:T(2,128)S(1)}, f32[3,68,2,256]{3,2,1,0:T(2,128)S(1)}, u32[]{:S(2)}, u32[]{:S(2)}) %collective-permute-start.11) | collective-permute-done | bytes 417824 | tf_op jit(solution)/shard_map/ppermute | solution.py:24
  207.3 3.1 %collective-permute-done.12 = f32[3,68,2,256]{3,2,1,0:T(2,128)S(1)} collective-permute-done((f32[3,68,2,256]{3,2,1,0:T(2,128)S(1)}, f32[3,68,2,256]{3,2,1,0:T(2,128)S(1)}, u32[]{:S(2)}, u32[]{:S(2)}) %collective-permute-start.12) | collective-permute-done | bytes 417824 | tf_op jit(solution)/shard_map/ppermute | solution.py:22
  210.5 1.3 pad_maximum_fusion.2
  211.8 4.9 %fusion.18 = f32[3,64,16,256]{3,2,1,0:T(8,128)} fusion(f32[3,68,18,256]{3,2,1,0:T(8,128)S(1)} %get-tuple-element.14, f32[3,68,18,256]{3,2,1,0:T(8,128)S(1)} %get-tuple-element.13, f32[3,64,16,256]{3,2,1,0:T(8,128)S(1)} %bitcast.45, f32[3,2,16,256]{3,2,1,0:T(8,128)S(1)} %collective-permute-done.10, f32[3,2,16,256]{3,2,1,0:T(8,128)} %copy-done.4, ...), kind=kLoop, calls=%fused_computation.47 | loop fusion | flops 18874368 | bytes 19072000 | tf_op jit(solution)/shard_map/add | solution.py:78
  216.6 2.3 fusion.48
  219.3 2.6 %fusion.56 = f32[3072,256]{1,0:T(8,128)S(1)} fusion(f32[3072,256]{1,0:T(8,128)S(1)} %bitcast.46, f32[256,256]{1,0:T(8,128)S(1)} %copy-done.2), kind=kOutput, calls=%fused_computation.118 | convolution fusion | flops 2415919104 | bytes 6553600 | tf_op jit(solution)/shard_map/dot_general | solution.py:83
  221.9 1.1 collective-permute-start.13
  223.0 1.0 collective-permute-start.14
  224.1 2.6 %collective-permute-done.13 = f32[3,2,16,256]{3,2,1,0:T(8,128)S(1)} collective-permute-done((f32[3,2,16,256]{3,2,1,0:T(8,128)S(1)}, f32[3,2,16,256]{3,2,1,0:T(8,128)S(1)}, u32[]{:S(2)}, u32[]{:S(2)}) %collective-permute-start.13) | collective-permute-done | bytes 98336 | tf_op jit(solution)/shard_map/ppermute | solution.py:22
  226.7 1.1 collective-permute-done.14
  228.6 5.0 %collective-permute-done.15 = f32[3,68,2,256]{3,2,1,0:T(2,128)S(1)} collective-permute-done((f32[3,68,2,256]{3,2,1,0:T(2,128)S(1)}, f32[3,68,2,256]{3,2,1,0:T(2,128)S(1)}, u32[]{:S(2)}, u32[]{:S(2)}) %collective-permute-start.15) | collective-permute-done | bytes 417824 | tf_op jit(solution)/shard_map/ppermute | solution.py:24
  233.6 3.1 %collective-permute-done.16 = f32[3,68,2,256]{3,2,1,0:T(2,128)S(1)} collective-permute-done((f32[3,68,2,256]{3,2,1,0:T(2,128)S(1)}, f32[3,68,2,256]{3,2,1,0:T(2,128)S(1)}, u32[]{:S(2)}, u32[]{:S(2)}) %collective-permute-start.16) | collective-permute-done | bytes 417824 | tf_op jit(solution)/shard_map/ppermute | solution.py:22
  236.7 1.3 pad_maximum_fusion.3
  238.0 4.1 %fusion.12 = f32[3,64,16,256]{3,2,1,0:T(8,128)} fusion(f32[3,68,18,256]{3,2,1,0:T(8,128)S(1)} %get-tuple-element.10, f32[3,68,18,256]{3,2,1,0:T(8,128)S(1)} %get-tuple-element.9, f32[3,64,16,256]{3,2,1,0:T(8,128)S(1)} %bitcast.37, f32[3,2,16,256]{3,2,1,0:T(8,128)S(1)} %collective-permute-done.14, f32[3,2,16,256]{3,2,1,0:T(8,128)S(1)} %collective-permute-done.13, ...), kind=kLoop, calls=%fused_computation.37 | loop fusion | flops 18874368 | bytes 19072000 | tf_op jit(solution)/shard_map/add | solution.py:78
  242.1 2.4 fusion.46
  244.5 4.3 %fusion.41 = f32[1,3,64,16,256]{4,3,2,1,0:T(8,128)} fusion(f32[256,256,1,1]{1,0,3,2:T(8,128)S(1)} %copy-done.5, f32[1,64,16,256]{3,2,1,0:T(8,128)S(1)} %get-tuple-element.26, f32[1,64,16,256]{3,2,1,0:T(8,128)S(1)} %get-tuple-element.27, f32[1,64,16,256]{3,2,1,0:T(8,128)S(1)} %get-tuple-element.25), kind=kOutput, calls=%fused_computation.87 | convolution fusion | flops 2417491968 | bytes 6553600 | tf_op jit(solution)/shard_map/dot_general | solution.py:83
  (37 shorter events, 3.3 us)
Async XLA Ops:
  0.0 139.1 %copy-start = (f32[1,3,64,16,256]{4,3,2,1,0:T(8,128)S(1)}, f32[1,3,64,16,256]{4,3,2,1,0:T(8,128)}, u32[]{:S(2)}) copy-start(f32[1,3,64,16,256]{4,3,2,1,0:T(8,128)} %param.8) | copy-start | bytes 9437188
  0.0 73.7 %collective-permute-start = (f32[1,3,64,16,256]{4,3,2,1,0:T(8,128)}, f32[1,3,64,16,256]{4,3,2,1,0:T(8,128)S(1)}, u32[]{:S(2)}, u32[]{:S(2)}) collective-permute-start(f32[1,3,64,16,256]{4,3,2,1,0:T(8,128)} %param.6), channel_id=1, source_target_pairs={{0,224},{32,0},{64,32},{96,64},{128,96},{160,128},{192,160},{224,1... | collective-permute-start | bytes 9437192 | tf_op jit(solution)/shard_map/ppermute | solution.py:34
  73.7 5.4 %copy-start.1 = (f32[1,3,64,16,256]{4,3,2,1,0:T(8,128)}, f32[1,3,64,16,256]{4,3,2,1,0:T(8,128)S(1)}, u32[]{:S(2)}) copy-start(f32[1,3,64,16,256]{4,3,2,1,0:T(8,128)S(1)} %collective-permute-done) | copy-start | bytes 9437188
  143.2 6.6 %copy-start.6 = (f32[256]{0:T(256)S(1)}, f32[256]{0:T(256)}, u32[]{:S(2)}) copy-start(f32[256]{0:T(256)} %param.9) | copy-start | bytes 3076
  143.2 6.6 %copy-start.7 = (f32[256]{0:T(256)S(1)}, f32[256]{0:T(256)}, u32[]{:S(2)}) copy-start(f32[256]{0:T(256)} %param.10) | copy-start | bytes 3076
  143.2 4.7 %collective-permute-start.1 = (f32[3,2,16,256]{3,2,1,0:T(8,128)S(1)}, f32[3,2,16,256]{3,2,1,0:T(8,128)S(1)}, u32[]{:S(2)}, u32[]{:S(2)}) collective-permute-start(f32[3,2,16,256]{3,2,1,0:T(8,128)S(1)} %get-tuple-element.43), channel_id=1, source_target_pairs={{0,16},{16,0},{1,17},{17,1},{2,18},{18,2},{3,19},{19,3},{4,20},{20... | collective-permute-start | bytes 294920 | tf_op jit(solution)/shard_map/ppermute | solution.py:22
  144.0 4.9 %collective-permute-start.2 = (f32[3,2,16,256]{3,2,1,0:T(8,128)S(1)}, f32[3,2,16,256]{3,2,1,0:T(8,128)S(1)}, u32[]{:S(2)}, u32[]{:S(2)}) collective-permute-start(f32[3,2,16,256]{3,2,1,0:T(8,128)S(1)} %get-tuple-element.44), channel_id=1, source_target_pairs={{16,0},{0,16},{17,1},{1,17},{18,2},{2,18},{19,3},{3,19},{20,4},{4,... | collective-permute-start | bytes 294920 | tf_op jit(solution)/shard_map/ppermute | solution.py:24
  149.3 5.6 %collective-permute-start.3 = (f32[3,68,2,256]{3,2,1,0:T(2,128)S(1)}, f32[3,68,2,256]{3,2,1,0:T(2,128)S(1)}, u32[]{:S(2)}, u32[]{:S(2)}) collective-permute-start(f32[3,68,2,256]{3,2,1,0:T(2,128)S(1)} %get-tuple-element.23), channel_id=1, source_target_pairs={{1,0},{2,1},{3,2},{4,3},{5,4},{6,5},{7,6},{8,7},{9,8},{10,9},{11,1... | collective-permute-start | bytes 1253384 | tf_op jit(solution)/shard_map/ppermute | solution.py:24
  149.3 8.7 %collective-permute-start.4 = (f32[3,68,2,256]{3,2,1,0:T(2,128)S(1)}, f32[3,68,2,256]{3,2,1,0:T(2,128)S(1)}, u32[]{:S(2)}, u32[]{:S(2)}) collective-permute-start(f32[3,68,2,256]{3,2,1,0:T(2,128)S(1)} %get-tuple-element.24), channel_id=1, source_target_pairs={{0,1},{1,2},{2,3},{3,4},{4,5},{5,6},{6,7},{7,8},{8,9},{9,10},{10,1... | collective-permute-start | bytes 1253384 | tf_op jit(solution)/shard_map/ppermute | solution.py:22
  165.7 1.0 copy-start.2
  169.3 4.7 %collective-permute-start.5 = (f32[3,2,16,256]{3,2,1,0:T(8,128)S(1)}, f32[3,2,16,256]{3,2,1,0:T(8,128)S(1)}, u32[]{:S(2)}, u32[]{:S(2)}) collective-permute-start(f32[3,2,16,256]{3,2,1,0:T(8,128)S(1)} %get-tuple-element.38), channel_id=1, source_target_pairs={{0,16},{16,0},{1,17},{17,1},{2,18},{18,2},{3,19},{19,3},{4,20},{20... | collective-permute-start | bytes 294920 | tf_op jit(solution)/shard_map/ppermute | solution.py:22
  170.4 4.7 %collective-permute-start.6 = (f32[3,2,16,256]{3,2,1,0:T(8,128)S(1)}, f32[3,2,16,256]{3,2,1,0:T(8,128)S(1)}, u32[]{:S(2)}, u32[]{:S(2)}) collective-permute-start(f32[3,2,16,256]{3,2,1,0:T(8,128)S(1)} %get-tuple-element.39), channel_id=1, source_target_pairs={{16,0},{0,16},{17,1},{1,17},{18,2},{2,18},{19,3},{3,19},{20,4},{4,... | collective-permute-start | bytes 294920 | tf_op jit(solution)/shard_map/ppermute | solution.py:24
  175.1 10.3 %copy-start.3 = (f32[3,2,16,256]{3,2,1,0:T(8,128)}, f32[3,2,16,256]{3,2,1,0:T(8,128)S(1)}, u32[]{:S(2)}) copy-start(f32[3,2,16,256]{3,2,1,0:T(8,128)S(1)} %collective-permute-done.6) | copy-start | bytes 294916
  175.4 5.6 %collective-permute-start.7 = (f32[3,68,2,256]{3,2,1,0:T(2,128)S(1)}, f32[3,68,2,256]{3,2,1,0:T(2,128)S(1)}, u32[]{:S(2)}, u32[]{:S(2)}) collective-permute-start(f32[3,68,2,256]{3,2,1,0:T(2,128)S(1)} %get-tuple-element.19), channel_id=1, source_target_pairs={{1,0},{2,1},{3,2},{4,3},{5,4},{6,5},{7,6},{8,7},{9,8},{10,9},{11,1... | collective-permute-start | bytes 1253384 | tf_op jit(solution)/shard_map/ppermute | solution.py:24
  175.4 8.7 %collective-permute-start.8 = (f32[3,68,2,256]{3,2,1,0:T(2,128)S(1)}, f32[3,68,2,256]{3,2,1,0:T(2,128)S(1)}, u32[]{:S(2)}, u32[]{:S(2)}) collective-permute-start(f32[3,68,2,256]{3,2,1,0:T(2,128)S(1)} %get-tuple-element.20), channel_id=1, source_target_pairs={{0,1},{1,2},{2,3},{3,4},{4,5},{5,6},{6,7},{7,8},{8,9},{9,10},{10,1... | collective-permute-start | bytes 1253384 | tf_op jit(solution)/shard_map/ppermute | solution.py:22
  195.7 4.7 %collective-permute-start.10 = (f32[3,2,16,256]{3,2,1,0:T(8,128)S(1)}, f32[3,2,16,256]{3,2,1,0:T(8,128)S(1)}, u32[]{:S(2)}, u32[]{:S(2)}) collective-permute-start(f32[3,2,16,256]{3,2,1,0:T(8,128)S(1)} %get-tuple-element.34), channel_id=1, source_target_pairs={{16,0},{0,16},{17,1},{1,17},{18,2},{2,18},{19,3},{3,19},{20,4},{4,... | collective-permute-start | bytes 294920 | tf_op jit(solution)/shard_map/ppermute | solution.py:24
  196.8 4.7 %collective-permute-start.9 = (f32[3,2,16,256]{3,2,1,0:T(8,128)S(1)}, f32[3,2,16,256]{3,2,1,0:T(8,128)S(1)}, u32[]{:S(2)}, u32[]{:S(2)}) collective-permute-start(f32[3,2,16,256]{3,2,1,0:T(8,128)S(1)} %get-tuple-element.33), channel_id=1, source_target_pairs={{0,16},{16,0},{1,17},{17,1},{2,18},{18,2},{3,19},{19,3},{4,20},{20... | collective-permute-start | bytes 294920 | tf_op jit(solution)/shard_map/ppermute | solution.py:22
  201.4 10.3 %copy-start.4 = (f32[3,2,16,256]{3,2,1,0:T(8,128)}, f32[3,2,16,256]{3,2,1,0:T(8,128)S(1)}, u32[]{:S(2)}) copy-start(f32[3,2,16,256]{3,2,1,0:T(8,128)S(1)} %collective-permute-done.9) | copy-start | bytes 294916
  201.7 5.6 %collective-permute-start.11 = (f32[3,68,2,256]{3,2,1,0:T(2,128)S(1)}, f32[3,68,2,256]{3,2,1,0:T(2,128)S(1)}, u32[]{:S(2)}, u32[]{:S(2)}) collective-permute-start(f32[3,68,2,256]{3,2,1,0:T(2,128)S(1)} %get-tuple-element.15), channel_id=1, source_target_pairs={{1,0},{2,1},{3,2},{4,3},{5,4},{6,5},{7,6},{8,7},{9,8},{10,9},{11,1... | collective-permute-start | bytes 1253384 | tf_op jit(solution)/shard_map/ppermute | solution.py:24
  201.8 8.7 %collective-permute-start.12 = (f32[3,68,2,256]{3,2,1,0:T(2,128)S(1)}, f32[3,68,2,256]{3,2,1,0:T(2,128)S(1)}, u32[]{:S(2)}, u32[]{:S(2)}) collective-permute-start(f32[3,68,2,256]{3,2,1,0:T(2,128)S(1)} %get-tuple-element.16), channel_id=1, source_target_pairs={{0,1},{1,2},{2,3},{3,4},{4,5},{5,6},{6,7},{7,8},{8,9},{9,10},{10,1... | collective-permute-start | bytes 1253384 | tf_op jit(solution)/shard_map/ppermute | solution.py:22
  221.9 4.7 %collective-permute-start.13 = (f32[3,2,16,256]{3,2,1,0:T(8,128)S(1)}, f32[3,2,16,256]{3,2,1,0:T(8,128)S(1)}, u32[]{:S(2)}, u32[]{:S(2)}) collective-permute-start(f32[3,2,16,256]{3,2,1,0:T(8,128)S(1)} %get-tuple-element.28), channel_id=1, source_target_pairs={{0,16},{16,0},{1,17},{17,1},{2,18},{18,2},{3,19},{19,3},{4,20},{20... | collective-permute-start | bytes 294920 | tf_op jit(solution)/shard_map/ppermute | solution.py:22
  223.0 4.7 %collective-permute-start.14 = (f32[3,2,16,256]{3,2,1,0:T(8,128)S(1)}, f32[3,2,16,256]{3,2,1,0:T(8,128)S(1)}, u32[]{:S(2)}, u32[]{:S(2)}) collective-permute-start(f32[3,2,16,256]{3,2,1,0:T(8,128)S(1)} %get-tuple-element.29), channel_id=1, source_target_pairs={{16,0},{0,16},{17,1},{1,17},{18,2},{2,18},{19,3},{3,19},{20,4},{4,... | collective-permute-start | bytes 294920 | tf_op jit(solution)/shard_map/ppermute | solution.py:24
  228.0 5.6 %collective-permute-start.15 = (f32[3,68,2,256]{3,2,1,0:T(2,128)S(1)}, f32[3,68,2,256]{3,2,1,0:T(2,128)S(1)}, u32[]{:S(2)}, u32[]{:S(2)}) collective-permute-start(f32[3,68,2,256]{3,2,1,0:T(2,128)S(1)} %get-tuple-element.11), channel_id=1, source_target_pairs={{1,0},{2,1},{3,2},{4,3},{5,4},{6,5},{7,6},{8,7},{9,8},{10,9},{11,1... | collective-permute-start | bytes 1253384 | tf_op jit(solution)/shard_map/ppermute | solution.py:24
  228.0 8.7 %collective-permute-start.16 = (f32[3,68,2,256]{3,2,1,0:T(2,128)S(1)}, f32[3,68,2,256]{3,2,1,0:T(2,128)S(1)}, u32[]{:S(2)}, u32[]{:S(2)}) collective-permute-start(f32[3,68,2,256]{3,2,1,0:T(2,128)S(1)} %get-tuple-element.12), channel_id=1, source_target_pairs={{0,1},{1,2},{2,3},{3,4},{4,5},{5,6},{6,7},{7,8},{8,9},{9,10},{10,1... | collective-permute-start | bytes 1253384 | tf_op jit(solution)/shard_map/ppermute | solution.py:22
  242.1 2.4 copy-start.5
where the time goes:
time: 249 us
  waiting for transfers between devices  120 us (48%)
  blocking collectives  58.7 us (24%)
  other arithmetic  44.1 us (18%)
  matrix products  12.1 us (5%)
  starting transfers between devices  10.8 us (4%)
    ppermute x1, waiting for transfers between devices, from_behind(): return lax.ppermute(value, axis, pairs)  73.3 us
    psum x1, blocking collectives, shards(): lax.psum((jnp.sum(started * direction), jnp.sum(direction * direction)),...  58.7 us
    ppermute x8, waiting for transfers between devices, with_halo(): lax.ppermute(head, axis, [((i + 1) % count, i) for i in range(count)])  25.7 us
    ppermute x8, waiting for transfers between devices, with_halo(): lax.ppermute(tail, axis, [(i, (i + 1) % count) for i in range(count)])  21.4 us
    add x4, other arithmetic, advance(): center + TIME_STEP * velocity * advect + DIFFUSE * (lap_x + lap_z)  18 us
    dot_general x4, matrix products, advance(): jnp.dot(flattened, table_t, precision=lax.Precision.HIGHEST, preferred_el...  12.1 us
    slice x4, other arithmetic, advance(): explicit[:1]  9.38 us
    ppermute x8, starting transfers between devices, with_halo(): lax.ppermute(tail, axis, [(i, (i + 1) % count) for i in range(count)])  5.99 us
  transfers between devices with their start and end apart: 17, of which 17 were waited for; matrix products, arithmetic and copies ran while one was open for 0% of the time, Pallas kernels for 0%

commit v1 on v0

--- a/solution.py
+++ b/solution.py
@@ -97,7 +97,7 @@
     started = received[0] + jump[0]
     direction = tangent[0]
     products = lax.psum(
-        (jnp.sum(started * direction), jnp.sum(direction * direction)), ("gx", "gz")
+        lax.psum((jnp.sum(started * direction), jnp.sum(direction * direction)), "gx"), "gz"
     )
     along_coef = products[0] / (products[1] + EPSILON)
     adjoint = started - along_coef * direction

time: 249 us -> 226 us (0.908)
  blocking collectives: 58.7 us -> 33.1 us
  waiting for transfers between devices: 120 us -> 123 us
    psum x1, blocking collectives: 58.7 us -> 5.62 us  [shards(): lax.psum((jnp.sum(started * direction), jnp.sum(direction * direction)),...]
    psum x0 -> x1, blocking collectives: none -> 27.5 us  [shards(): lax.psum(lax.psum((jnp.sum(started * direction), jnp.sum(direction * dire...]
where the time goes in v1:
time: 226 us; the launch traced here: 225 us
  waiting for transfers between devices  123 us (54%)
  other arithmetic  44.1 us (20%)
  blocking collectives  33.1 us (15%)
  matrix products  12.1 us (5%)
  starting transfers between devices  10.9 us (5%)
    ppermute x1, waiting for transfers between devices, from_behind(): return lax.ppermute(value, axis, pairs)  73.3 us
    psum x1, blocking collectives, shards(): lax.psum(lax.psum((jnp.sum(started * direction), jnp.sum(direction * dire...  27.5 us
    ppermute x8, waiting for transfers between devices, with_halo(): lax.ppermute(head, axis, [((i + 1) % count, i) for i in range(count)])  27.3 us
    ppermute x8, waiting for transfers between devices, with_halo(): lax.ppermute(tail, axis, [(i, (i + 1) % count) for i in range(count)])  22.3 us
    add x4, other arithmetic, advance(): center + TIME_STEP * velocity * advect + DIFFUSE * (lap_x + lap_z)  18 us
    dot_general x4, matrix products, advance(): jnp.dot(flattened, table_t, precision=lax.Precision.HIGHEST, preferred_el...  12.1 us
    slice x4, other arithmetic, advance(): explicit[:1]  9.38 us
    ppermute x8, starting transfers between devices, with_halo(): lax.ppermute(tail, axis, [(i, (i + 1) % count) for i in range(count)])  5.83 us
  transfers between devices with their start and end apart: 17, of which 17 were waited for; matrix products, arithmetic and copies ran while one was open for 0% of the time, Pallas kernels for 0%

profile of v1, /device:TPU:22, one launch (start us, length us, event | category | flops | bytes accessed | tf_op | source)
XLA Modules:
  0.0 225.5 jit_solution(18263741179743924742)
XLA Ops:
  0.3 73.3 %collective-permute-done = f32[1,3,64,16,256]{4,3,2,1,0:T(8,128)S(1)} collective-permute-done((f32[1,3,64,16,256]{4,3,2,1,0:T(8,128)}, f32[1,3,64,16,256]{4,3,2,1,0:T(8,128)S(1)}, u32[]{:S(2)}, u32[]{:S(2)}) %collective-permute-start) | collective-permute-done | bytes 3145760 | tf_op jit(solution)/shard_map/ppermute | solution.py:34
  73.7 5.4 %fusion.39 = (f32[]{:T(128)}, f32[]{:T(128)}) fusion(f32[1,3,64,16,256]{4,3,2,1,0:T(8,128)} %param.8, f32[1,3,64,16,256]{4,3,2,1,0:T(8,128)S(1)} %collective-permute-done, f32[1,3,64,16,256]{4,3,2,1,0:T(8,128)} %param.7), kind=kLoop, calls=%fused_computation.85 | loop fusion | flops 3932158 | bytes 9437192 | tf_op jit(solution)/shard_map/reduce_sum | solution.py:100
  79.1 5.6 %all-reduce.1 = (f32[]{:T(128)}, f32[]{:T(128)}) all-reduce(f32[]{:T(128)} %get-tuple-element.6, f32[]{:T(128)} %get-tuple-element.5), channel_id=1, replica_groups=mesh['seg'=8,'gx'=2,'gz'=16] {'gx'}, use_global_device_ids=true, to_apply=%region_1.0 | all-reduce | flops 2 | bytes 16 | tf_op jit(solution)/shard_map/psum | solution.py:100
  84.7 27.5 %all-reduce = (f32[]{:T(128)}, f32[]{:T(128)}) all-reduce(f32[]{:T(128)} %get-tuple-element.9, f32[]{:T(128)} %get-tuple-element.10), channel_id=1, replica_groups=mesh['seg'=8,'gx'=2,'gz'=16] {'gz'}, use_global_device_ids=true, to_apply=%region_2.0 | all-reduce | flops 2 | bytes 16 | tf_op jit(solution)/shard_map/psum | solution.py:99
  113.4 4.0 %fusion.40 = f32[3,64,16,256]{3,2,1,0:T(8,128)S(1)} fusion(f32[1,3,64,16,256]{4,3,2,1,0:T(8,128)S(1)} %copy-done, f32[]{:T(128)S(6)} %div.31, f32[1,3,64,16,256]{4,3,2,1,0:T(8,128)} %copy-done.1, f32[1,3,64,16,256]{4,3,2,1,0:T(8,128)} %param.7), kind=kLoop, calls=%fused_computation.86 | loop fusion | flops 2359296 | bytes 12582916 | tf_op jit(solution)/shard_map/sub | solution.py:103
  117.4 1.4 collective-permute-start.1
  118.8 0.7 collective-permute-start.2
  119.5 3.3 %collective-permute-done.1 = f32[3,2,16,256]{3,2,1,0:T(8,128)S(1)} collective-permute-done((f32[3,2,16,256]{3,2,1,0:T(8,128)S(1)}, f32[3,2,16,256]{3,2,1,0:T(8,128)S(1)}, u32[]{:S(2)}, u32[]{:S(2)}) %collective-permute-start.1) | collective-permute-done | bytes 98336 | tf_op jit(solution)/shard_map/ppermute | solution.py:22
  122.9 1.1 collective-permute-done.2
  124.3 0.5 collective-permute-start.4
  124.8 5.0 %collective-permute-done.3 = f32[3,68,2,256]{3,2,1,0:T(2,128)S(1)} collective-permute-done((f32[3,68,2,256]{3,2,1,0:T(2,128)S(1)}, f32[3,68,2,256]{3,2,1,0:T(2,128)S(1)}, u32[]{:S(2)}, u32[]{:S(2)}) %collective-permute-start.3) | collective-permute-done | bytes 417824 | tf_op jit(solution)/shard_map/ppermute | solution.py:24
  129.8 3.1 %collective-permute-done.4 = f32[3,68,2,256]{3,2,1,0:T(2,128)S(1)} collective-permute-done((f32[3,68,2,256]{3,2,1,0:T(2,128)S(1)}, f32[3,68,2,256]{3,2,1,0:T(2,128)S(1)}, u32[]{:S(2)}, u32[]{:S(2)}) %collective-permute-start.4) | collective-permute-done | bytes 417824 | tf_op jit(solution)/shard_map/ppermute | solution.py:22
  132.9 1.3 pad_maximum_fusion
  134.3 4.1 %fusion.30 = f32[3,64,16,256]{3,2,1,0:T(8,128)} fusion(f32[3,68,18,256]{3,2,1,0:T(8,128)S(1)} %get-tuple-element.24, f32[3,68,18,256]{3,2,1,0:T(8,128)S(1)} %get-tuple-element.23, f32[3,64,16,256]{3,2,1,0:T(8,128)S(1)} %fusion.40, f32[3,2,16,256]{3,2,1,0:T(8,128)S(1)} %collective-permute-done.2, f32[3,2,16,256]{3,2,1,0:T(8,128)S(1)} %collective-permute-done.1, ...), kind=kLoop, calls=%fused_computation.67 | loop fusion | flops 18874368 | bytes 19072000 | tf_op jit(solution)/shard_map/add | solution.py:78
  138.3 2.3 %fusion.52 = (f32[1,64,16,256]{3,2,1,0:T(8,128)S(1)}, f32[1,64,16,256]{3,2,1,0:T(8,128)S(1)}, f32[1,64,16,256]{3,2,1,0:T(8,128)S(1)}) fusion(f32[3,64,16,256]{3,2,1,0:T(8,128)} %fusion.30, f32[3,64,16,256]{3,2,1,0:T(8,128)S(1)} %fusion.40, f32[256]{0:T(256)S(1)} %broadcast_multiply_fusion), kind=kLoop, calls=%fused_computation.114 | loop fusion | flops 524288 | bytes 7341056 | tf_op jit(solution)/shard_map/slice | solution.py:80
  141.0 0.6 copy-done.2
  141.6 2.6 %fusion.54 = f32[3072,256]{1,0:T(8,128)S(1)} fusion(f32[3072,256]{1,0:T(8,128)S(1)} %bitcast.47, f32[256,256]{1,0:T(8,128)S(1)} %copy-done.2), kind=kOutput, calls=%fused_computation.116 | convolution fusion | flops 2415919104 | bytes 6553600 | tf_op jit(solution)/shard_map/dot_general | solution.py:83
  144.3 1.4 collective-permute-start.5
  145.7 0.7 collective-permute-start.6
  146.4 2.6 %collective-permute-done.5 = f32[3,2,16,256]{3,2,1,0:T(8,128)S(1)} collective-permute-done((f32[3,2,16,256]{3,2,1,0:T(8,128)S(1)}, f32[3,2,16,256]{3,2,1,0:T(8,128)S(1)}, u32[]{:S(2)}, u32[]{:S(2)}) %collective-permute-start.5) | collective-permute-done | bytes 98336 | tf_op jit(solution)/shard_map/ppermute | solution.py:22
  149.0 1.3 collective-permute-done.6
  151.2 5.3 %collective-permute-done.7 = f32[3,68,2,256]{3,2,1,0:T(2,128)S(1)} collective-permute-done((f32[3,68,2,256]{3,2,1,0:T(2,128)S(1)}, f32[3,68,2,256]{3,2,1,0:T(2,128)S(1)}, u32[]{:S(2)}, u32[]{:S(2)}) %collective-permute-start.7) | collective-permute-done | bytes 417824 | tf_op jit(solution)/shard_map/ppermute | solution.py:24
  156.5 3.1 %collective-permute-done.8 = f32[3,68,2,256]{3,2,1,0:T(2,128)S(1)} collective-permute-done((f32[3,68,2,256]{3,2,1,0:T(2,128)S(1)}, f32[3,68,2,256]{3,2,1,0:T(2,128)S(1)}, u32[]{:S(2)}, u32[]{:S(2)}) %collective-permute-start.8) | collective-permute-done | bytes 417824 | tf_op jit(solution)/shard_map/ppermute | solution.py:22
  159.6 1.3 pad_maximum_fusion.1
  160.9 5.0 %fusion.24 = f32[3,64,16,256]{3,2,1,0:T(8,128)} fusion(f32[3,68,18,256]{3,2,1,0:T(8,128)S(1)} %get-tuple-element.20, f32[3,68,18,256]{3,2,1,0:T(8,128)S(1)} %get-tuple-element.19, f32[3,64,16,256]{3,2,1,0:T(8,128)S(1)} %bitcast.41, f32[3,2,16,256]{3,2,1,0:T(8,128)} %copy-done.3, f32[3,2,16,256]{3,2,1,0:T(8,128)S(1)} %collective-permute-done.5, ...), kind=kLoop, calls=%fused_computation.57 | loop fusion | flops 18874368 | bytes 19072000 | tf_op jit(solution)/shard_map/add | solution.py:78
  165.9 2.3 %fusion.50 = (f32[1,64,16,256]{3,2,1,0:T(8,128)S(1)}, f32[1,64,16,256]{3,2,1,0:T(8,128)S(1)}, f32[1,64,16,256]{3,2,1,0:T(8,128)S(1)}) fusion(f32[3,64,16,256]{3,2,1,0:T(8,128)} %fusion.24, f32[1,64,16,256]{3,2,1,0:T(8,128)S(1)} %bitcast.50, f32[256]{0:T(256)S(1)} %broadcast_multiply_fusion), kind=kLoop, calls=%fused_computation.112 | loop fusion | flops 524288 | bytes 7341056 | tf_op jit(solution)/shard_map/slice | solution.py:80
  168.5 2.6 %fusion.55 = f32[3072,256]{1,0:T(8,128)S(1)} fusion(f32[3072,256]{1,0:T(8,128)S(1)} %bitcast.48, f32[256,256]{1,0:T(8,128)S(1)} %copy-done.2), kind=kOutput, calls=%fused_computation.117 | convolution fusion | flops 2415919104 | bytes 6553600 | tf_op jit(solution)/shard_map/dot_general | solution.py:83
  171.2 1.4 collective-permute-start.10
  172.6 0.7 collective-permute-start.9
  173.3 2.6 %collective-permute-done.10 = f32[3,2,16,256]{3,2,1,0:T(8,128)S(1)} collective-permute-done((f32[3,2,16,256]{3,2,1,0:T(8,128)S(1)}, f32[3,2,16,256]{3,2,1,0:T(8,128)S(1)}, u32[]{:S(2)}, u32[]{:S(2)}) %collective-permute-start.10) | collective-permute-done | bytes 98336 | tf_op jit(solution)/shard_map/ppermute | solution.py:24
  175.9 1.3 collective-permute-done.9
  177.5 0.4 collective-permute-start.11
  178.1 5.4 %collective-permute-done.11 = f32[3,68,2,256]{3,2,1,0:T(2,128)S(1)} collective-permute-done((f32[3,68,2,256]{3,2,1,0:T(2,128)S(1)}, f32[3,68,2,256]{3,2,1,0:T(2,128)S(1)}, u32[]{:S(2)}, u32[]{:S(2)}) %collective-permute-start.11) | collective-permute-done | bytes 417824 | tf_op jit(solution)/shard_map/ppermute | solution.py:24
  183.4 3.1 %collective-permute-done.12 = f32[3,68,2,256]{3,2,1,0:T(2,128)S(1)} collective-permute-done((f32[3,68,2,256]{3,2,1,0:T(2,128)S(1)}, f32[3,68,2,256]{3,2,1,0:T(2,128)S(1)}, u32[]{:S(2)}, u32[]{:S(2)}) %collective-permute-start.12) | collective-permute-done | bytes 417824 | tf_op jit(solution)/shard_map/ppermute | solution.py:22
  186.6 1.3 pad_maximum_fusion.2
  187.9 4.9 %fusion.18 = f32[3,64,16,256]{3,2,1,0:T(8,128)} fusion(f32[3,68,18,256]{3,2,1,0:T(8,128)S(1)} %get-tuple-element.16, f32[3,68,18,256]{3,2,1,0:T(8,128)S(1)} %get-tuple-element.15, f32[3,64,16,256]{3,2,1,0:T(8,128)S(1)} %bitcast.45, f32[3,2,16,256]{3,2,1,0:T(8,128)S(1)} %collective-permute-done.10, f32[3,2,16,256]{3,2,1,0:T(8,128)} %copy-done.4, ...), kind=kLoop, calls=%fused_computation.47 | loop fusion | flops 18874368 | bytes 19072000 | tf_op jit(solution)/shard_map/add | solution.py:78
  192.7 2.3 %fusion.48 = (f32[1,64,16,256]{3,2,1,0:T(8,128)S(1)}, f32[1,64,16,256]{3,2,1,0:T(8,128)S(1)}, f32[1,64,16,256]{3,2,1,0:T(8,128)S(1)}) fusion(f32[3,64,16,256]{3,2,1,0:T(8,128)} %fusion.18, f32[1,64,16,256]{3,2,1,0:T(8,128)S(1)} %bitcast.51, f32[256]{0:T(256)S(1)} %broadcast_multiply_fusion), kind=kLoop, calls=%fused_computation.110 | loop fusion | flops 524288 | bytes 7341056 | tf_op jit(solution)/shard_map/slice | solution.py:80
  195.4 2.6 %fusion.56 = f32[3072,256]{1,0:T(8,128)S(1)} fusion(f32[3072,256]{1,0:T(8,128)S(1)} %bitcast.46, f32[256,256]{1,0:T(8,128)S(1)} %copy-done.2), kind=kOutput, calls=%fused_computation.118 | convolution fusion | flops 2415919104 | bytes 6553600 | tf_op jit(solution)/shard_map/dot_general | solution.py:83
  198.1 1.4 collective-permute-start.13
  199.5 0.7 collective-permute-start.14
  200.2 2.6 %collective-permute-done.13 = f32[3,2,16,256]{3,2,1,0:T(8,128)S(1)} collective-permute-done((f32[3,2,16,256]{3,2,1,0:T(8,128)S(1)}, f32[3,2,16,256]{3,2,1,0:T(8,128)S(1)}, u32[]{:S(2)}, u32[]{:S(2)}) %collective-permute-start.13) | collective-permute-done | bytes 98336 | tf_op jit(solution)/shard_map/ppermute | solution.py:22
  202.8 1.3 collective-permute-done.14
  205.0 5.3 %collective-permute-done.15 = f32[3,68,2,256]{3,2,1,0:T(2,128)S(1)} collective-permute-done((f32[3,68,2,256]{3,2,1,0:T(2,128)S(1)}, f32[3,68,2,256]{3,2,1,0:T(2,128)S(1)}, u32[]{:S(2)}, u32[]{:S(2)}) %collective-permute-start.15) | collective-permute-done | bytes 417824 | tf_op jit(solution)/shard_map/ppermute | solution.py:24
  210.3 3.1 %collective-permute-done.16 = f32[3,68,2,256]{3,2,1,0:T(2,128)S(1)} collective-permute-done((f32[3,68,2,256]{3,2,1,0:T(2,128)S(1)}, f32[3,68,2,256]{3,2,1,0:T(2,128)S(1)}, u32[]{:S(2)}, u32[]{:S(2)}) %collective-permute-start.16) | collective-permute-done | bytes 417824 | tf_op jit(solution)/shard_map/ppermute | solution.py:22
  213.4 1.3 pad_maximum_fusion.3
  214.7 4.1 %fusion.12 = f32[3,64,16,256]{3,2,1,0:T(8,128)} fusion(f32[3,68,18,256]{3,2,1,0:T(8,128)S(1)} %get-tuple-element.12, f32[3,68,18,256]{3,2,1,0:T(8,128)S(1)} %get-tuple-element.11, f32[3,64,16,256]{3,2,1,0:T(8,128)S(1)} %bitcast.37, f32[3,2,16,256]{3,2,1,0:T(8,128)S(1)} %collective-permute-done.14, f32[3,2,16,256]{3,2,1,0:T(8,128)S(1)} %collective-permute-done.13, ...), kind=kLoop, calls=%fused_computation.37 | loop fusion | flops 18874368 | bytes 19072000 | tf_op jit(solution)/shard_map/add | solution.py:78
  218.8 2.4 %fusion.46 = (f32[1,64,16,256]{3,2,1,0:T(8,128)S(1)}, f32[1,64,16,256]{3,2,1,0:T(8,128)S(1)}, f32[1,64,16,256]{3,2,1,0:T(8,128)S(1)}) fusion(f32[3,64,16,256]{3,2,1,0:T(8,128)} %fusion.12, f32[1,64,16,256]{3,2,1,0:T(8,128)S(1)} %bitcast.49, f32[256]{0:T(256)S(1)} %broadcast_multiply_fusion), kind=kLoop, calls=%fused_computation.108 | loop fusion | flops 524288 | bytes 7341056 | tf_op jit(solution)/shard_map/slice | solution.py:80
  221.2 4.3 %fusion.41 = f32[1,3,64,16,256]{4,3,2,1,0:T(8,128)} fusion(f32[256,256,1,1]{1,0,3,2:T(8,128)S(1)} %copy-done.5, f32[1,64,16,256]{3,2,1,0:T(8,128)S(1)} %get-tuple-element.28, f32[1,64,16,256]{3,2,1,0:T(8,128)S(1)} %get-tuple-element.29, f32[1,64,16,256]{3,2,1,0:T(8,128)S(1)} %get-tuple-element.27), kind=kOutput, calls=%fused_computation.87 | convolution fusion | flops 2417491968 | bytes 6553600 | tf_op jit(solution)/shard_map/dot_general | solution.py:83
  (38 shorter events, 3.9 us)
Async XLA Ops:
  0.0 113.4 %copy-start = (f32[1,3,64,16,256]{4,3,2,1,0:T(8,128)S(1)}, f32[1,3,64,16,256]{4,3,2,1,0:T(8,128)}, u32[]{:S(2)}) copy-start(f32[1,3,64,16,256]{4,3,2,1,0:T(8,128)} %param.8) | copy-start | bytes 9437188
  0.0 73.7 %collective-permute-start = (f32[1,3,64,16,256]{4,3,2,1,0:T(8,128)}, f32[1,3,64,16,256]{4,3,2,1,0:T(8,128)S(1)}, u32[]{:S(2)}, u32[]{:S(2)}) collective-permute-start(f32[1,3,64,16,256]{4,3,2,1,0:T(8,128)} %param.6), channel_id=1, source_target_pairs={{0,224},{32,0},{64,32},{96,64},{128,96},{160,128},{192,160},{224,1... | collective-permute-start | bytes 9437192 | tf_op jit(solution)/shard_map/ppermute | solution.py:34
  73.7 5.4 %copy-start.1 = (f32[1,3,64,16,256]{4,3,2,1,0:T(8,128)}, f32[1,3,64,16,256]{4,3,2,1,0:T(8,128)S(1)}, u32[]{:S(2)}) copy-start(f32[1,3,64,16,256]{4,3,2,1,0:T(8,128)S(1)} %collective-permute-done) | copy-start | bytes 9437188
  117.4 7.4 %copy-start.6 = (f32[256]{0:T(256)S(1)}, f32[256]{0:T(256)}, u32[]{:S(2)}) copy-start(f32[256]{0:T(256)} %param.9) | copy-start | bytes 3076
  117.4 7.4 %copy-start.7 = (f32[256]{0:T(256)S(1)}, f32[256]{0:T(256)}, u32[]{:S(2)}) copy-start(f32[256]{0:T(256)} %param.10) | copy-start | bytes 3076
  117.4 5.5 %collective-permute-start.1 = (f32[3,2,16,256]{3,2,1,0:T(8,128)S(1)}, f32[3,2,16,256]{3,2,1,0:T(8,128)S(1)}, u32[]{:S(2)}, u32[]{:S(2)}) collective-permute-start(f32[3,2,16,256]{3,2,1,0:T(8,128)S(1)} %get-tuple-element.45), channel_id=1, source_target_pairs={{0,16},{16,0},{1,17},{17,1},{2,18},{18,2},{3,19},{19,3},{4,20},{20... | collective-permute-start | bytes 294920 | tf_op jit(solution)/shard_map/ppermute | solution.py:22
  118.8 5.1 %collective-permute-start.2 = (f32[3,2,16,256]{3,2,1,0:T(8,128)S(1)}, f32[3,2,16,256]{3,2,1,0:T(8,128)S(1)}, u32[]{:S(2)}, u32[]{:S(2)}) collective-permute-start(f32[3,2,16,256]{3,2,1,0:T(8,128)S(1)} %get-tuple-element.46), channel_id=1, source_target_pairs={{16,0},{0,16},{17,1},{1,17},{18,2},{2,18},{19,3},{3,19},{20,4},{4,... | collective-permute-start | bytes 294920 | tf_op jit(solution)/shard_map/ppermute | solution.py:24
  124.2 5.6 %collective-permute-start.3 = (f32[3,68,2,256]{3,2,1,0:T(2,128)S(1)}, f32[3,68,2,256]{3,2,1,0:T(2,128)S(1)}, u32[]{:S(2)}, u32[]{:S(2)}) collective-permute-start(f32[3,68,2,256]{3,2,1,0:T(2,128)S(1)} %get-tuple-element.25), channel_id=1, source_target_pairs={{1,0},{2,1},{3,2},{4,3},{5,4},{6,5},{7,6},{8,7},{9,8},{10,9},{11,1... | collective-permute-start | bytes 1253384 | tf_op jit(solution)/shard_map/ppermute | solution.py:24
  124.3 8.7 %collective-permute-start.4 = (f32[3,68,2,256]{3,2,1,0:T(2,128)S(1)}, f32[3,68,2,256]{3,2,1,0:T(2,128)S(1)}, u32[]{:S(2)}, u32[]{:S(2)}) collective-permute-start(f32[3,68,2,256]{3,2,1,0:T(2,128)S(1)} %get-tuple-element.26), channel_id=1, source_target_pairs={{0,1},{1,2},{2,3},{3,4},{4,5},{5,6},{6,7},{7,8},{8,9},{9,10},{10,1... | collective-permute-start | bytes 1253384 | tf_op jit(solution)/shard_map/ppermute | solution.py:22
  140.7 1.0 copy-start.2
  144.3 4.7 %collective-permute-start.5 = (f32[3,2,16,256]{3,2,1,0:T(8,128)S(1)}, f32[3,2,16,256]{3,2,1,0:T(8,128)S(1)}, u32[]{:S(2)}, u32[]{:S(2)}) collective-permute-start(f32[3,2,16,256]{3,2,1,0:T(8,128)S(1)} %get-tuple-element.40), channel_id=1, source_target_pairs={{0,16},{16,0},{1,17},{17,1},{2,18},{18,2},{3,19},{19,3},{4,20},{20... | collective-permute-start | bytes 294920 | tf_op jit(solution)/shard_map/ppermute | solution.py:22
  145.7 4.6 %collective-permute-start.6 = (f32[3,2,16,256]{3,2,1,0:T(8,128)S(1)}, f32[3,2,16,256]{3,2,1,0:T(8,128)S(1)}, u32[]{:S(2)}, u32[]{:S(2)}) collective-permute-start(f32[3,2,16,256]{3,2,1,0:T(8,128)S(1)} %get-tuple-element.41), channel_id=1, source_target_pairs={{16,0},{0,16},{17,1},{1,17},{18,2},{2,18},{19,3},{3,19},{20,4},{4,... | collective-permute-start | bytes 294920 | tf_op jit(solution)/shard_map/ppermute | solution.py:24
  150.3 10.6 %copy-start.3 = (f32[3,2,16,256]{3,2,1,0:T(8,128)}, f32[3,2,16,256]{3,2,1,0:T(8,128)S(1)}, u32[]{:S(2)}) copy-start(f32[3,2,16,256]{3,2,1,0:T(8,128)S(1)} %collective-permute-done.6) | copy-start | bytes 294916
  150.6 5.9 %collective-permute-start.7 = (f32[3,68,2,256]{3,2,1,0:T(2,128)S(1)}, f32[3,68,2,256]{3,2,1,0:T(2,128)S(1)}, u32[]{:S(2)}, u32[]{:S(2)}) collective-permute-start(f32[3,68,2,256]{3,2,1,0:T(2,128)S(1)} %get-tuple-element.21), channel_id=1, source_target_pairs={{1,0},{2,1},{3,2},{4,3},{5,4},{6,5},{7,6},{8,7},{9,8},{10,9},{11,1... | collective-permute-start | bytes 1253384 | tf_op jit(solution)/shard_map/ppermute | solution.py:24
  150.9 8.7 %collective-permute-start.8 = (f32[3,68,2,256]{3,2,1,0:T(2,128)S(1)}, f32[3,68,2,256]{3,2,1,0:T(2,128)S(1)}, u32[]{:S(2)}, u32[]{:S(2)}) collective-permute-start(f32[3,68,2,256]{3,2,1,0:T(2,128)S(1)} %get-tuple-element.22), channel_id=1, source_target_pairs={{0,1},{1,2},{2,3},{3,4},{4,5},{5,6},{6,7},{7,8},{8,9},{9,10},{10,1... | collective-permute-start | bytes 1253384 | tf_op jit(solution)/shard_map/ppermute | solution.py:22
  171.2 4.7 %collective-permute-start.10 = (f32[3,2,16,256]{3,2,1,0:T(8,128)S(1)}, f32[3,2,16,256]{3,2,1,0:T(8,128)S(1)}, u32[]{:S(2)}, u32[]{:S(2)}) collective-permute-start(f32[3,2,16,256]{3,2,1,0:T(8,128)S(1)} %get-tuple-element.36), channel_id=1, source_target_pairs={{16,0},{0,16},{17,1},{1,17},{18,2},{2,18},{19,3},{3,19},{20,4},{4,... | collective-permute-start | bytes 294920 | tf_op jit(solution)/shard_map/ppermute | solution.py:24
  172.6 4.6 %collective-permute-start.9 = (f32[3,2,16,256]{3,2,1,0:T(8,128)S(1)}, f32[3,2,16,256]{3,2,1,0:T(8,128)S(1)}, u32[]{:S(2)}, u32[]{:S(2)}) collective-permute-start(f32[3,2,16,256]{3,2,1,0:T(8,128)S(1)} %get-tuple-element.35), channel_id=1, source_target_pairs={{0,16},{16,0},{1,17},{17,1},{2,18},{18,2},{3,19},{19,3},{4,20},{20... | collective-permute-start | bytes 294920 | tf_op jit(solution)/shard_map/ppermute | solution.py:22
  177.2 10.7 %copy-start.4 = (f32[3,2,16,256]{3,2,1,0:T(8,128)}, f32[3,2,16,256]{3,2,1,0:T(8,128)S(1)}, u32[]{:S(2)}) copy-start(f32[3,2,16,256]{3,2,1,0:T(8,128)S(1)} %collective-permute-done.9) | copy-start | bytes 294916
  177.5 5.9 %collective-permute-start.11 = (f32[3,68,2,256]{3,2,1,0:T(2,128)S(1)}, f32[3,68,2,256]{3,2,1,0:T(2,128)S(1)}, u32[]{:S(2)}, u32[]{:S(2)}) collective-permute-start(f32[3,68,2,256]{3,2,1,0:T(2,128)S(1)} %get-tuple-element.17), channel_id=1, source_target_pairs={{1,0},{2,1},{3,2},{4,3},{5,4},{6,5},{7,6},{8,7},{9,8},{10,9},{11,1... | collective-permute-start | bytes 1253384 | tf_op jit(solution)/shard_map/ppermute | solution.py:24
  177.9 8.7 %collective-permute-start.12 = (f32[3,68,2,256]{3,2,1,0:T(2,128)S(1)}, f32[3,68,2,256]{3,2,1,0:T(2,128)S(1)}, u32[]{:S(2)}, u32[]{:S(2)}) collective-permute-start(f32[3,68,2,256]{3,2,1,0:T(2,128)S(1)} %get-tuple-element.18), channel_id=1, source_target_pairs={{0,1},{1,2},{2,3},{3,4},{4,5},{5,6},{6,7},{7,8},{8,9},{9,10},{10,1... | collective-permute-start | bytes 1253384 | tf_op jit(solution)/shard_map/ppermute | solution.py:22
  198.1 4.7 %collective-permute-start.13 = (f32[3,2,16,256]{3,2,1,0:T(8,128)S(1)}, f32[3,2,16,256]{3,2,1,0:T(8,128)S(1)}, u32[]{:S(2)}, u32[]{:S(2)}) collective-permute-start(f32[3,2,16,256]{3,2,1,0:T(8,128)S(1)} %get-tuple-element.30), channel_id=1, source_target_pairs={{0,16},{16,0},{1,17},{17,1},{2,18},{18,2},{3,19},{19,3},{4,20},{20... | collective-permute-start | bytes 294920 | tf_op jit(solution)/shard_map/ppermute | solution.py:22
  199.5 4.6 %collective-permute-start.14 = (f32[3,2,16,256]{3,2,1,0:T(8,128)S(1)}, f32[3,2,16,256]{3,2,1,0:T(8,128)S(1)}, u32[]{:S(2)}, u32[]{:S(2)}) collective-permute-start(f32[3,2,16,256]{3,2,1,0:T(8,128)S(1)} %get-tuple-element.31), channel_id=1, source_target_pairs={{16,0},{0,16},{17,1},{1,17},{18,2},{2,18},{19,3},{3,19},{20,4},{4,... | collective-permute-start | bytes 294920 | tf_op jit(solution)/shard_map/ppermute | solution.py:24
  204.4 5.9 %collective-permute-start.15 = (f32[3,68,2,256]{3,2,1,0:T(2,128)S(1)}, f32[3,68,2,256]{3,2,1,0:T(2,128)S(1)}, u32[]{:S(2)}, u32[]{:S(2)}) collective-permute-start(f32[3,68,2,256]{3,2,1,0:T(2,128)S(1)} %get-tuple-element.13), channel_id=1, source_target_pairs={{1,0},{2,1},{3,2},{4,3},{5,4},{6,5},{7,6},{8,7},{9,8},{10,9},{11,1... | collective-permute-start | bytes 1253384 | tf_op jit(solution)/shard_map/ppermute | solution.py:24
  204.7 8.7 %collective-permute-start.16 = (f32[3,68,2,256]{3,2,1,0:T(2,128)S(1)}, f32[3,68,2,256]{3,2,1,0:T(2,128)S(1)}, u32[]{:S(2)}, u32[]{:S(2)}) collective-permute-start(f32[3,68,2,256]{3,2,1,0:T(2,128)S(1)} %get-tuple-element.14), channel_id=1, source_target_pairs={{0,1},{1,2},{2,3},{3,4},{4,5},{5,6},{6,7},{7,8},{8,9},{9,10},{10,1... | collective-permute-start | bytes 1253384 | tf_op jit(solution)/shard_map/ppermute | solution.py:22
  218.8 2.4 %copy-start.5 = (f32[256,256,1,1]{1,0,3,2:T(8,128)S(1)}, f32[256,256,1,1]{1,0,3,2:T(8,128)}, u32[]{:S(2)}) copy-start(f32[256,256,1,1]{1,0,3,2:T(8,128)} %constant.40) | copy-start | bytes 786436
